TPU v7x, 32 devices: a whole 2x2x4 slice. The times are simulated.
32 devices in a mesh: row: 4 (over y, core), col: 8 (over z, x).
Axes of the slice: x: 2, y: 2, z: 4, core: 2. Of those that a mesh axis runs over, the one named last changes fastest.
Arguments:
- points: bfloat16 [65536, 512], P(('row', 'col')), may hold values from -6 to 6
- factor: bfloat16 [65536, 2048], P(('row', 'col')), may hold values from -0.078125 to 0.078125
- targets: bfloat16 [65536, 256], P(('row', 'col')), may hold values from -6 to 6
- pivot_slots: int32 [32, 32], P(('row', 'col')), may hold values from 0 to 2047, as said below
- pivot_counts: int32 [32], replicated, may hold values from 1 to 32, 512 in all
Outputs:
- new_columns: bfloat16 [512, 65536], P(None, ('row', 'col'))
- residual_next: float32 [65536, 256], P(('row', 'col'))
Inputs may be any that keep to these rules, and one draw needn't show every extreme that they name: `pivot_slots`: each row holds 32 different local row numbers; row d's first pivot_counts[d] entries are device d's pivots, the rest are unused. `pivot_counts`: the counts sum to 512; one of them is 32.
All inputs are finite; a program needn't handle non-finite values.
Results may differ from a plain program's by a relative error of at most 0.0029.
Values may be sent and summed in bfloat16 or wider, within the bound.
No kernel may reach another device: no remote copies, remote signals or barrier semaphores. Data moves between devices by JAX's collectives and lax.ppermute only.
A program may use at most 128 MiB of HBM per device.

v0:
```python
import jax
import jax.numpy as jnp
from jax import lax
from jax.sharding import PartitionSpec as P

BLOCK = 512
sharpness = 1.0
ridge_shift = 0.01
damping = 1.0
epsilon = 1e-06


def normalize(points):
    values = points.astype(jnp.float32)
    factor_scale = lax.rsqrt(jnp.mean(values * values, axis=1, keepdims=True) + epsilon)
    return (values * factor_scale).astype(jnp.bfloat16)


def kernel(left_rows, right_rows, feature_width):
    cosine = (
        lax.dot_general(
            left_rows, right_rows, (((1,), (1,)), ((), ())), preferred_element_type=jnp.float32
        )
        / feature_width
    )
    return jnp.exp(sharpness * (cosine - 1.0))


def compact_index(pivot_counts, block_size):
    owners_count = pivot_counts.shape[0]
    run_ends = jnp.cumsum(pivot_counts)
    run_starts = run_ends - pivot_counts
    position = jnp.arange(block_size, dtype=jnp.int32)
    owners = jnp.sum((position[:, None] >= run_ends[None, :]).astype(jnp.int32), axis=1)
    onehot = (owners[:, None] == jnp.arange(owners_count, dtype=jnp.int32)[None, :]).astype(
        jnp.int32
    )
    first_row = jnp.sum(onehot * run_starts[None, :], axis=1)
    return (owners, position - first_row)


def block_factor(pivot_scaled, pivot_factor):
    intersection = lax.dot_general(
        pivot_factor, pivot_factor, (((1,), (1,)), ((), ())), preferred_element_type=jnp.float32
    )
    diag_shift = ridge_shift + jnp.max(jnp.sum(jnp.abs(intersection), axis=1))
    ridged = (
        kernel(pivot_scaled, pivot_scaled, pivot_scaled.shape[1])
        - intersection
        + diag_shift * jnp.eye(intersection.shape[0], dtype=jnp.float32)
    )
    return jnp.linalg.cholesky(ridged)


def on_device(points, factor, targets, pivot_slots, pivot_counts):
    scaled = normalize(points)
    local_slots = pivot_slots[0]
    slot_cap = pivot_slots.shape[1]
    own_scaled = jnp.take(scaled, local_slots, axis=0)
    own_factor = jnp.take(factor, local_slots, axis=0)
    inner_scaled, inner_factor = (
        lax.all_gather(own_scaled, "col", axis=0, tiled=True),
        lax.all_gather(own_factor, "col", axis=0, tiled=True),
    )
    padded_scaled, padded_factor = (
        lax.all_gather(inner_scaled, "row", axis=0, tiled=True),
        lax.all_gather(inner_factor, "row", axis=0, tiled=True),
    )
    owners, slot_index = compact_index(pivot_counts, BLOCK)
    row_index = owners * slot_cap + slot_index
    pivot_scaled = jnp.take(padded_scaled, row_index, axis=0)
    pivot_factor = jnp.take(padded_factor, row_index, axis=0)
    lower_factor = block_factor(pivot_scaled, pivot_factor)
    downdated = kernel(pivot_scaled, scaled, scaled.shape[1]) - lax.dot_general(
        pivot_factor, factor, (((1,), (1,)), ((), ())), preferred_element_type=jnp.float32
    )
    new_columns = lax.linalg.triangular_solve(
        lower_factor, downdated, left_side=True, lower=True
    ).astype(jnp.bfloat16)
    cross_terms = jnp.concatenate(
        [
            lax.dot_general(
                factor, targets, (((0,), (0,)), ((), ())), preferred_element_type=jnp.float32
            ),
            lax.dot_general(
                new_columns, targets, (((1,), (0,)), ((), ())), preferred_element_type=jnp.float32
            ),
        ],
        axis=0,
    )
    col_norms = jnp.concatenate(
        [
            jnp.sum(jnp.square(factor.astype(jnp.float32)), axis=0),
            jnp.sum(jnp.square(new_columns.astype(jnp.float32)), axis=1),
        ],
        axis=0,
    )
    cross_whole, norm_whole = lax.psum((cross_terms, col_norms), ("row", "col"))
    coefficients = (cross_whole / (norm_whole + damping)[:, None]).astype(jnp.bfloat16)
    held_count = factor.shape[1]
    fitted = jnp.dot(factor, coefficients[:held_count], preferred_element_type=jnp.float32)
    fitted = fitted + lax.dot_general(
        new_columns,
        coefficients[held_count:],
        (((0,), (0,)), ((), ())),
        preferred_element_type=jnp.float32,
    )
    residual_next = targets.astype(jnp.float32) - fitted
    return (new_columns, residual_next)


def solution(mesh):
    return jax.shard_map(
        on_device,
        mesh=mesh,
        in_specs=(
            P(("row", "col"), None),
            P(("row", "col"), None),
            P(("row", "col"), None),
            P(("row", "col"), None),
            P(),
        ),
        out_specs=(P(None, ("row", "col")), P(("row", "col"), None)),
        check_vma=False,
    )
```

profile of v0, /device:TPU:0, one launch (start us, length us, event | category | flops | bytes accessed | tf_op | source)
XLA Modules:
  0.0 457.6 jit_solution(8331831617520132772)
XLA Ops:
  7.2 0.7 fusion.40
  7.9 0.7 compare_and_fusion
  8.5 5.2 %gather_fusion.2 = bf16[32,2048]{1,0:T(8,128)(2,1)S(1)} fusion(bf16[2048,2048]{1,0:T(8,128)(2,1)} %param.6, s32[1024]{0:T(1024)S(1)} %pad_clamp_fusion.1), kind=kCustom, calls=%fused_computation.2 | custom fusion | bytes 262272 | tf_op jit(solution)/shard_map/jit(_take)/gather | solution.py:60
  13.8 0.7 broadcast_select_fusion.6
  14.6 2.2 fusion
  17.3 0.6 gather_fusion
  18.0 35.1 %all_gather.12 = bf16[256,512]{1,0:T(8,128)(2,1)} all-gather(bf16[32,512]{1,0:T(8,128)(2,1)S(1)} %broadcast_select_fusion.7), channel_id=1, replica_groups=mesh['row'=4,'col'=8] {'col'}, dimensions={0}, use_global_device_ids=true | all-gather | bytes 294912 | tf_op jit(solution)/shard_map/all_gather | solution.py:62
  53.2 5.6 %all-gather.6.cloned.1.call-done = bf16[256,2048]{1,0:T(8,128)(2,1)} async-done(((bf16[32,2048]{1,0:T(8,128)(2,1)}), bf16[256,2048]{1,0:T(8,128)(2,1)}) %all-gather.6.cloned.1.call-update) | async-done | bytes 1048592 | tf_op jit(solution)/shard_map/all_gather | solution.py:63
  59.5 7.2 %fusion.51 = f32[2048,256]{1,0:T(8,128)} fusion(bf16[2048,2048]{1,0:T(8,128)(2,1)} %param.6, bf16[2048,256]{1,0:T(8,128)(2,1)S(1)} %copy-done.6), kind=kOutput, calls=%fused_computation.122 | convolution fusion | flops 2147483648 | bytes 11534336 | tf_op jit(solution)/shard_map/dot_general | solution.py:82
  66.7 9.0 %all-gather.4.cloned.1.call-done = bf16[1024,512]{1,0:T(8,128)(2,1)} async-done(((bf16[256,512]{1,0:T(8,128)(2,1)}), bf16[1024,512]{1,0:T(8,128)(2,1)}) %all-gather.4.cloned.1.call-update) | async-done | bytes 1048592 | tf_op jit(solution)/shard_map/all_gather | solution.py:66
  75.7 4.0 gather_fusion.1
  79.7 32.0 %all-gather.8.cloned.1.call-done = bf16[1024,2048]{1,0:T(8,128)(2,1)} async-done(((bf16[256,2048]{1,0:T(8,128)(2,1)}), bf16[1024,2048]{1,0:T(8,128)(2,1)}) %all-gather.8.cloned.1.call-update) | async-done | bytes 4194320 | tf_op jit(solution)/shard_map/all_gather | solution.py:67
  111.8 8.0 %gather_fusion.3 = bf16[512,2048]{1,0:T(8,128)(2,1)} fusion(bf16[1024,2048]{1,0:T(8,128)(2,1)} %all-gather.8.cloned.1.call-done, s32[1024]{0:T(1024)S(1)} %pad_clamp_fusion), kind=kCustom, calls=%fused_computation.3 | custom fusion | bytes 4196352 | tf_op jit(solution)/shard_map/jit(_take)/gather | solution.py:72
  119.7 3.7 abs_reduce_fusion
  123.5 9.9 %fusion.21 = f32[512,2048]{1,0:T(8,128)} fusion(bf16[2048,2048]{1,0:T(8,128)(2,1)} %param.6, bf16[512,2048]{1,0:T(8,128)(2,1)S(1)} %copy-done.4, pred[512]{0:T(512)(128)(4,1)S(1)} %compare_and_fusion.1), kind=kOutput, calls=%fused_computation.51 | convolution fusion | flops 4296015872 | bytes 14680576 | tf_op jit(solution)/shard_map/dot_general | solution.py:74
  133.3 1.3 copy.20
  134.6 2.1 fusion.17
  136.8 1.3 copy.21
  138.1 0.6 reduce_max.9
  139.3 1.4 add_multiply_fusion
  140.8 1.0 copy-done.3
  141.8 11.7 %cholesky.103 = f32[128,128]{1,0:T(8,128)S(1)} custom-call(f32[128,128]{1,0:T(8,128)S(1)} %cholesky.263), custom_call_target="Cholesky" | custom-call | tf_op jit(solution)/shard_map/jit(cholesky)/cholesky | solution.py:52
  153.7 9.8 %custom-call.30 = f32[1,128,128]{1,2,0:T(8,128)S(1)} custom-call(f32[1,128,128]{2,1,0:T(8,128)S(1)} %get-tuple-element.37), custom_call_target="InvertDiagBlocksLowerTriangular" | custom-call | tf_op jit(solution)/shard_map/jit(cholesky)/cholesky | solution.py:52
  163.5 1.2 constant_dynamic-update-slice_fusion.3
  164.7 1.3 convolution_subtract_fusion.2
  166.0 11.7 %cholesky.215 = f32[128,128]{1,0:T(8,128)S(1)} custom-call(f32[128,128]{1,0:T(8,128)S(1)} %cholesky.267), custom_call_target="Cholesky" | custom-call | tf_op jit(solution)/shard_map/jit(cholesky)/cholesky | solution.py:52
  177.8 10.2 %custom-call.31 = f32[1,128,128]{1,2,0:T(8,128)S(1)} custom-call(f32[1,128,128]{2,1,0:T(8,128)S(1)} %get-tuple-element.34), custom_call_target="InvertDiagBlocksLowerTriangular" | custom-call | tf_op jit(solution)/shard_map/jit(cholesky)/cholesky | solution.py:52
  188.3 1.3 convolution_subtract_fusion.3
  189.6 11.7 %cholesky.236 = f32[128,128]{1,0:T(8,128)S(1)} custom-call(f32[128,128]{1,0:T(8,128)S(1)} %cholesky.272), custom_call_target="Cholesky" | custom-call | tf_op jit(solution)/shard_map/jit(cholesky)/cholesky | solution.py:52
  201.3 0.7 compare_reduce_fusion.1
  202.0 9.8 %custom-call.32 = f32[1,128,128]{1,2,0:T(8,128)S(1)} custom-call(f32[1,128,128]{2,1,0:T(8,128)S(1)} %get-tuple-element.31), custom_call_target="InvertDiagBlocksLowerTriangular" | custom-call | tf_op jit(solution)/shard_map/jit(cholesky)/cholesky | solution.py:52
  212.0 1.2 convolution_subtract_fusion.4
  213.2 11.8 %cholesky.253 = f32[128,128]{1,0:T(8,128)S(1)} custom-call(f32[128,128]{1,0:T(8,128)S(1)} %convolution_subtract_fusion.4), custom_call_target="Cholesky" | custom-call | tf_op jit(solution)/shard_map/jit(cholesky)/cholesky | solution.py:52
  225.1 0.6 compare_reduce_fusion
  225.7 0.6 compare_reduce_fusion.2
  228.8 1.1 select_select_fusion
  229.9 13.6 %while.1 = (s32[]{:T(128)}, f32[512,512]{1,0:T(8,128)}, s32[4,2]{0,1:T(2,128)S(1)}, f32[4,128,128]{2,1,0:T(8,128)}, s32[]{:T(128)}) while((s32[]{:T(128)}, f32[512,512]{1,0:T(8,128)}, s32[4,2]{0,1:T(2,128)S(1)}, f32[4,128,128]{2,1,0:T(8,128)}, s32[]{:T(128)}) %tuple.39), condition=%wide.while_cond, body=%wide.while_body.sunk | while | flops 2 | bytes 132705 | solution.py:77
  230.0 0.5 fusion.67
  230.6 2.8 bitcast_dynamic-update-slice_fusion.2
  233.5 0.5 fusion.67
  234.0 2.8 bitcast_dynamic-update-slice_fusion.2
  237.4 2.8 bitcast_dynamic-update-slice_fusion.2
  240.8 2.7 bitcast_dynamic-update-slice_fusion.2
  243.6 40.1 %custom-call.33 = f32[4,128,128]{1,2,0:T(8,128)S(1)} custom-call(f32[4,128,128]{2,1,0:T(8,128)} %get-tuple-element.9), custom_call_target="InvertDiagBlocksLowerTriangular" | custom-call | tf_op jit(solution)/shard_map/triangular_solve | solution.py:77
  283.7 3.7 exponential_subtract_fusion
  287.4 1.1 fusion.50
  288.5 1.9 convolution_subtract_fusion.1
  290.4 1.0 fusion.49
  291.4 2.2 convolution_subtract_fusion
  293.6 1.0 fusion.48
  294.7 3.0 fusion.9
  297.7 1.1 convolution_convert_fusion
  298.8 0.6 multiply_reduce_fusion.1
  299.4 1.3 copy-done
  300.7 0.7 fusion.52
  301.7 1.7 pad_maximum_fusion
  303.4 0.9 copy.22
  304.3 5.1 %multiply_reduce_fusion = f32[2048]{0:T(1024)S(1)} fusion(bf16[2048,2048]{1,0:T(8,128)(2,1)} %param.6), kind=kLoop, calls=%fused_computation.6 | loop fusion | flops 12580864 | bytes 8396800 | tf_op jit(solution)/shard_map/reduce_sum | solution.py:93
  309.4 39.6 %psum.15 = f32[2560]{0:T(1024)S(1)} all-reduce(f32[2560]{0:T(1024)S(1)} %pad_maximum_fusion.2), channel_id=1, replica_groups=mesh['row'=4,'col'=8] {'row','col'}, use_global_device_ids=true, to_apply=%region_17.18 | all-reduce | flops 2560 | bytes 20480 | tf_op jit(solution)/shard_map/psum | solution.py:98
  349.0 91.1 %all-reduce.3.cloned.1.call-done = f32[2560,256]{1,0:T(8,128)} async-done(((f32[2560,256]{1,0:T(8,128)}), f32[2560,256]{1,0:T(8,128)}) %all-reduce.3.cloned.1.call-update) | async-done | bytes 2621456 | tf_op jit(solution)/shard_map/psum | solution.py:98
  440.1 2.1 divide_convert_fusion
  442.3 5.9 %convolution_bitcast_fusion = f32[2048,256]{0,1:T(8,128)S(1)} fusion(bf16[2048,2048]{1,0:T(8,128)(2,1)} %param.6, bf16[2560,256]{1,0:T(8,128)(2,1)S(1)} %divide_convert_fusion), kind=kOutput, calls=%fused_computation.21 | convolution fusion | flops 2147483648 | bytes 11534336 | tf_op jit(solution)/shard_map/dot_general | solution.py:101
  448.2 0.8 fusion.8
  449.0 1.8 copy.24
  (59 shorter events, 3.9 us)
Async XLA Ops:
  7.2 51.6 %all-gather.6.cloned.1.call-start = ((), (), s32[]{:S(2)}) async-start(), calls=%async_computation.1 | async-start | bytes 1179648 | tf_op jit(solution)/shard_map/all_gather | solution.py:63
  14.5 61.2 %all-gather.4.cloned.1.call-start = ((), (), s32[]{:S(2)}) async-start(), calls=%async_computation | async-start | bytes 1310720 | tf_op jit(solution)/shard_map/all_gather | solution.py:66
  14.6 2.3 copy-start.2
  16.8 42.1 %copy-start.8 = (s32[32]{0:T(128)S(1)}, s32[32]{0:T(128)}, u32[]{:S(2)}) copy-start(s32[32]{0:T(128)} %param.9) | copy-start | bytes 388
  16.9 42.7 %copy-start.6 = (bf16[2048,256]{1,0:T(8,128)(2,1)S(1)}, bf16[2048,256]{1,0:T(8,128)(2,1)}, u32[]{:S(2)}) copy-start(bf16[2048,256]{1,0:T(8,128)(2,1)} %param.7) | copy-start | bytes 3145732
  53.1 58.6 %all-gather.8.cloned.1.call-start = ((), (), s32[]{:S(2)}) async-start(), calls=%async_computation.2 | async-start | bytes 5242880 | tf_op jit(solution)/shard_map/all_gather | solution.py:67
  58.8 381.4 %all-reduce.3.cloned.1.call-start = ((), (), s32[]{:S(2)}) async-start(), calls=%async_computation.3 | async-start | bytes 5242880 | tf_op jit(solution)/shard_map/psum | solution.py:98
  119.7 3.8 copy-start.4
  140.8 1.0 copy-start.3
  297.7 3.0 copy-start.7
  299.4 1.3 copy-start
  299.4 2.3 copy-start.5
  442.3 5.9 %copy-start.1 = (bf16[512,2048]{1,0:T(8,128)(2,1)S(1)}, bf16[512,2048]{1,0:T(8,128)(2,1)}, u32[]{:S(2)}) copy-start(bf16[512,2048]{1,0:T(8,128)(2,1)} %copy-done) | copy-start | bytes 6291460
Sparse Core Ops, SparseCore 0:
  14.7 44.0 all-gather.5
  60.3 15.3 all-gather.3
  77.3 34.4 all-gather.7
  303.6 136.5 all-reduce.2
where the time goes:
time: 461 us; the launch traced here: 458 us
  waiting for transfers between devices  138 us (30%)
  other arithmetic  137 us (30%)
  blocking collectives  74.7 us (16%)
  matrix products  50.8 us (11%)
  local copies, waits for them, and re-layouts  39.5 us (9%)
  between operations  17.5 us (4%)
    psum x1, waiting for transfers between devices, on_device(): cross_whole, norm_whole = lax.psum((cross_terms, col_norms), ('row', 'col'))  91.1 us
    another operation x14, other arithmetic, block_factor(): return jnp.linalg.cholesky(ridged)  78.9 us
    another operation x3, other arithmetic, on_device(): lax.linalg.triangular_solve(lower_factor, downdated, left_side=True, lowe...  41.2 us
    psum x1, blocking collectives, on_device(): cross_whole, norm_whole = lax.psum((cross_terms, col_norms), ('row', 'col'))  39.6 us
    all_gather x1, blocking collectives, on_device(): lax.all_gather(own_scaled, 'col', axis=0, tiled=True)  35.1 us
    all_gather x1, waiting for transfers between devices, on_device(): lax.all_gather(inner_factor, 'row', axis=0, tiled=True)  32 us
    another operation x13, local copies, waits for them, and re-layouts  13.7 us
    another operation x7, matrix products, on_device(): lax.linalg.triangular_solve(lower_factor, downdated, left_side=True, lowe...  11.3 us
  transfers between devices with their start and end apart: 4, of which 4 were waited for; matrix products, arithmetic and copies ran while one was open for 5% of the time, Pallas kernels for 0%

commit v1 on v0

--- a/solution.py
+++ b/solution.py
@@ -8,6 +8,11 @@
 ridge_shift = 0.01
 damping = 1.0
 epsilon = 1e-06
+
+
+def by_each_axis(array, inner_axis, outer_axis):
+    half = lax.psum(array, inner_axis)
+    return lax.psum(half, outer_axis)
 
 
 def normalize(points):
@@ -95,7 +100,7 @@
         ],
         axis=0,
     )
-    cross_whole, norm_whole = lax.psum((cross_terms, col_norms), ("row", "col"))
+    cross_whole, norm_whole = by_each_axis((cross_terms, col_norms), "row", "col")
     coefficients = (cross_whole / (norm_whole + damping)[:, None]).astype(jnp.bfloat16)
     held_count = factor.shape[1]
     fitted = jnp.dot(factor, coefficients[:held_count], preferred_element_type=jnp.float32)

time: 461 us -> 505 us (1.095)
  waiting for transfers between devices: 138 us -> 172 us
  blocking collectives: 74.7 us -> 84.1 us
    psum x1 -> x2, waiting for transfers between devices: 91.1 us -> 125 us  [the longest x1 65.2 us: by_each_axis(): return lax.psum(half, outer_axis)]
    psum x1 -> x2, blocking collectives: 39.6 us -> 49 us  [the longest x1 38.5 us: by_each_axis(): return lax.psum(half, outer_axis)]
  transfers between devices with their start and end apart: 4 -> 5, of which waited for: 4 -> 5; matrix products, arithmetic and copies ran while one was open for 5% -> 4% of each run, Pallas kernels for 0% -> 0%
where the time goes in v1:
time: 505 us; the launch traced here: 501 us
  waiting for transfers between devices  172 us (34%)
  other arithmetic  137 us (27%)
  blocking collectives  84.1 us (17%)
  matrix products  50.8 us (10%)
  local copies, waits for them, and re-layouts  39.5 us (8%)
  between operations  17.5 us (3%)
    another operation x14, other arithmetic, block_factor(): return jnp.linalg.cholesky(ridged)  78.9 us
    psum x1, waiting for transfers between devices, by_each_axis(): return lax.psum(half, outer_axis)  65.2 us
    psum x1, waiting for transfers between devices, by_each_axis(): half = lax.psum(array, inner_axis)  60 us
    another operation x3, other arithmetic, on_device(): lax.linalg.triangular_solve(lower_factor, downdated, left_side=True, lowe...  41.2 us
    psum x1, blocking collectives, by_each_axis(): return lax.psum(half, outer_axis)  38.5 us
    all_gather x1, blocking collectives, on_device(): lax.all_gather(own_scaled, 'col', axis=0, tiled=True)  35.1 us
    all_gather x1, waiting for transfers between devices, on_device(): lax.all_gather(inner_factor, 'row', axis=0, tiled=True)  32 us
    another operation x13, local copies, waits for them, and re-layouts  13.7 us
  transfers between devices with their start and end apart: 5, of which 5 were waited for; matrix products, arithmetic and copies ran while one was open for 4% of the time, Pallas kernels for 0%

profile of v1, /device:TPU:0, one launch (start us, length us, event | category | flops | bytes accessed | tf_op | source)
XLA Modules:
  0.0 501.2 jit_solution(12826020302805920670)
XLA Ops:
  7.2 0.7 fusion.40
  7.9 0.7 compare_and_fusion
  8.5 5.2 %gather_fusion.2 = bf16[32,2048]{1,0:T(8,128)(2,1)S(1)} fusion(bf16[2048,2048]{1,0:T(8,128)(2,1)} %param.6, s32[1024]{0:T(1024)S(1)} %pad_clamp_fusion.1), kind=kCustom, calls=%fused_computation.2 | custom fusion | bytes 262272 | tf_op jit(solution)/shard_map/jit(_take)/gather | solution.py:65
  13.8 0.7 broadcast_select_fusion.6
  14.6 2.2 fusion
  17.3 0.6 gather_fusion
  18.0 35.1 %all_gather.12 = bf16[256,512]{1,0:T(8,128)(2,1)} all-gather(bf16[32,512]{1,0:T(8,128)(2,1)S(1)} %broadcast_select_fusion.7), channel_id=1, replica_groups=mesh['row'=4,'col'=8] {'col'}, dimensions={0}, use_global_device_ids=true | all-gather | bytes 294912 | tf_op jit(solution)/shard_map/all_gather | solution.py:67
  53.2 5.6 %all-gather.6.cloned.1.call-done = bf16[256,2048]{1,0:T(8,128)(2,1)} async-done(((bf16[32,2048]{1,0:T(8,128)(2,1)}), bf16[256,2048]{1,0:T(8,128)(2,1)}) %all-gather.6.cloned.1.call-update) | async-done | bytes 1048592 | tf_op jit(solution)/shard_map/all_gather | solution.py:68
  59.5 7.2 %fusion.51 = f32[2048,256]{1,0:T(8,128)} fusion(bf16[2048,2048]{1,0:T(8,128)(2,1)} %param.6, bf16[2048,256]{1,0:T(8,128)(2,1)S(1)} %copy-done.6), kind=kOutput, calls=%fused_computation.122 | convolution fusion | flops 2147483648 | bytes 11534336 | tf_op jit(solution)/shard_map/dot_general | solution.py:87
  66.7 9.0 %all-gather.4.cloned.1.call-done = bf16[1024,512]{1,0:T(8,128)(2,1)} async-done(((bf16[256,512]{1,0:T(8,128)(2,1)}), bf16[1024,512]{1,0:T(8,128)(2,1)}) %all-gather.4.cloned.1.call-update) | async-done | bytes 1048592 | tf_op jit(solution)/shard_map/all_gather | solution.py:71
  75.7 4.0 gather_fusion.1
  79.7 32.0 %all-gather.8.cloned.1.call-done = bf16[1024,2048]{1,0:T(8,128)(2,1)} async-done(((bf16[256,2048]{1,0:T(8,128)(2,1)}), bf16[1024,2048]{1,0:T(8,128)(2,1)}) %all-gather.8.cloned.1.call-update) | async-done | bytes 4194320 | tf_op jit(solution)/shard_map/all_gather | solution.py:72
  111.8 8.0 %gather_fusion.3 = bf16[512,2048]{1,0:T(8,128)(2,1)} fusion(bf16[1024,2048]{1,0:T(8,128)(2,1)} %all-gather.8.cloned.1.call-done, s32[1024]{0:T(1024)S(1)} %pad_clamp_fusion), kind=kCustom, calls=%fused_computation.3 | custom fusion | bytes 4196352 | tf_op jit(solution)/shard_map/jit(_take)/gather | solution.py:77
  119.7 3.7 abs_reduce_fusion
  123.5 9.9 %fusion.21 = f32[512,2048]{1,0:T(8,128)} fusion(bf16[2048,2048]{1,0:T(8,128)(2,1)} %param.6, bf16[512,2048]{1,0:T(8,128)(2,1)S(1)} %copy-done.4, pred[512]{0:T(512)(128)(4,1)S(1)} %compare_and_fusion.1), kind=kOutput, calls=%fused_computation.51 | convolution fusion | flops 4296015872 | bytes 14680576 | tf_op jit(solution)/shard_map/dot_general | solution.py:79
  133.3 1.3 copy.20
  134.6 2.1 fusion.17
  136.8 1.3 copy.21
  138.1 0.6 reduce_max.9
  139.3 1.4 add_multiply_fusion
  140.8 1.0 copy-done.3
  141.8 11.7 %cholesky.103 = f32[128,128]{1,0:T(8,128)S(1)} custom-call(f32[128,128]{1,0:T(8,128)S(1)} %cholesky.263), custom_call_target="Cholesky" | custom-call | tf_op jit(solution)/shard_map/jit(cholesky)/cholesky | solution.py:57
  153.7 9.8 %custom-call.30 = f32[1,128,128]{1,2,0:T(8,128)S(1)} custom-call(f32[1,128,128]{2,1,0:T(8,128)S(1)} %get-tuple-element.37), custom_call_target="InvertDiagBlocksLowerTriangular" | custom-call | tf_op jit(solution)/shard_map/jit(cholesky)/cholesky | solution.py:57
  163.5 1.2 constant_dynamic-update-slice_fusion.3
  164.7 1.3 convolution_subtract_fusion.2
  166.0 11.7 %cholesky.215 = f32[128,128]{1,0:T(8,128)S(1)} custom-call(f32[128,128]{1,0:T(8,128)S(1)} %cholesky.267), custom_call_target="Cholesky" | custom-call | tf_op jit(solution)/shard_map/jit(cholesky)/cholesky | solution.py:57
  177.8 10.2 %custom-call.31 = f32[1,128,128]{1,2,0:T(8,128)S(1)} custom-call(f32[1,128,128]{2,1,0:T(8,128)S(1)} %get-tuple-element.34), custom_call_target="InvertDiagBlocksLowerTriangular" | custom-call | tf_op jit(solution)/shard_map/jit(cholesky)/cholesky | solution.py:57
  188.3 1.3 convolution_subtract_fusion.3
  189.6 11.7 %cholesky.236 = f32[128,128]{1,0:T(8,128)S(1)} custom-call(f32[128,128]{1,0:T(8,128)S(1)} %cholesky.272), custom_call_target="Cholesky" | custom-call | tf_op jit(solution)/shard_map/jit(cholesky)/cholesky | solution.py:57
  201.3 0.7 compare_reduce_fusion.1
  202.0 9.8 %custom-call.32 = f32[1,128,128]{1,2,0:T(8,128)S(1)} custom-call(f32[1,128,128]{2,1,0:T(8,128)S(1)} %get-tuple-element.31), custom_call_target="InvertDiagBlocksLowerTriangular" | custom-call | tf_op jit(solution)/shard_map/jit(cholesky)/cholesky | solution.py:57
  212.0 1.2 convolution_subtract_fusion.4
  213.2 11.8 %cholesky.253 = f32[128,128]{1,0:T(8,128)S(1)} custom-call(f32[128,128]{1,0:T(8,128)S(1)} %convolution_subtract_fusion.4), custom_call_target="Cholesky" | custom-call | tf_op jit(solution)/shard_map/jit(cholesky)/cholesky | solution.py:57
  225.1 0.6 compare_reduce_fusion
  225.7 0.6 compare_reduce_fusion.2
  228.8 1.1 select_select_fusion
  229.9 13.6 %while.1 = (s32[]{:T(128)}, f32[512,512]{1,0:T(8,128)}, s32[4,2]{0,1:T(2,128)S(1)}, f32[4,128,128]{2,1,0:T(8,128)}, s32[]{:T(128)}) while((s32[]{:T(128)}, f32[512,512]{1,0:T(8,128)}, s32[4,2]{0,1:T(2,128)S(1)}, f32[4,128,128]{2,1,0:T(8,128)}, s32[]{:T(128)}) %tuple.39), condition=%wide.while_cond, body=%wide.while_body.sunk | while | flops 2 | bytes 132705 | solution.py:82
  230.6 2.8 bitcast_dynamic-update-slice_fusion.2
  234.0 2.8 bitcast_dynamic-update-slice_fusion.2
  237.4 2.8 bitcast_dynamic-update-slice_fusion.2
  240.8 2.7 bitcast_dynamic-update-slice_fusion.2
  243.6 40.1 %custom-call.33 = f32[4,128,128]{1,2,0:T(8,128)S(1)} custom-call(f32[4,128,128]{2,1,0:T(8,128)} %get-tuple-element.9), custom_call_target="InvertDiagBlocksLowerTriangular" | custom-call | tf_op jit(solution)/shard_map/triangular_solve | solution.py:82
  283.7 3.7 exponential_subtract_fusion
  287.4 1.1 fusion.50
  288.5 1.9 convolution_subtract_fusion.1
  290.4 1.0 fusion.49
  291.4 2.2 convolution_subtract_fusion
  293.6 1.0 fusion.48
  294.7 3.0 fusion.9
  297.7 1.1 convolution_convert_fusion
  298.8 0.6 multiply_reduce_fusion.1
  299.4 1.3 copy-done
  300.7 0.7 fusion.52
  301.7 1.7 pad_maximum_fusion
  303.5 60.0 %all-reduce.4.cloned.1.call-done = f32[2560,256]{1,0:T(8,128)} async-done(((f32[2560,256]{1,0:T(8,128)}), f32[2560,256]{1,0:T(8,128)}) %all-reduce.4.cloned.1.call-update) | async-done | bytes 2621456 | tf_op jit(solution)/shard_map/psum | solution.py:14
  363.5 0.9 copy.22
  364.4 5.1 %multiply_reduce_fusion = f32[2048]{0:T(1024)S(1)} fusion(bf16[2048,2048]{1,0:T(8,128)(2,1)} %param.6), kind=kLoop, calls=%fused_computation.6 | loop fusion | flops 12580864 | bytes 8396800 | tf_op jit(solution)/shard_map/reduce_sum | solution.py:98
  369.5 10.5 %psum.30 = f32[2560]{0:T(1024)S(1)} all-reduce(f32[2560]{0:T(1024)S(1)} %pad_maximum_fusion.2), channel_id=1, replica_groups=mesh['row'=4,'col'=8] {'row'}, use_global_device_ids=true, to_apply=%region_18.19 | all-reduce | flops 2560 | bytes 20480 | tf_op jit(solution)/shard_map/psum | solution.py:14
  380.0 38.5 %psum.31 = f32[2560]{0:T(1024)S(1)} all-reduce(f32[2560]{0:T(1024)S(1)} %psum.30), channel_id=1, replica_groups=mesh['row'=4,'col'=8] {'col'}, use_global_device_ids=true, to_apply=%region_19.20 | all-reduce | flops 2560 | bytes 20480 | tf_op jit(solution)/shard_map/psum | solution.py:15
  418.5 65.2 %all-reduce.6.cloned.1.call-done = f32[2560,256]{1,0:T(8,128)} async-done(((f32[2560,256]{1,0:T(8,128)}), f32[2560,256]{1,0:T(8,128)}) %all-reduce.6.cloned.1.call-update) | async-done | bytes 2621456 | tf_op jit(solution)/shard_map/psum | solution.py:15
  483.8 2.1 divide_convert_fusion
  485.9 5.9 %convolution_bitcast_fusion = f32[2048,256]{0,1:T(8,128)S(1)} fusion(bf16[2048,2048]{1,0:T(8,128)(2,1)} %param.6, bf16[2560,256]{1,0:T(8,128)(2,1)S(1)} %divide_convert_fusion), kind=kOutput, calls=%fused_computation.21 | convolution fusion | flops 2147483648 | bytes 11534336 | tf_op jit(solution)/shard_map/dot_general | solution.py:106
  491.9 0.8 fusion.8
  492.6 1.8 copy.24
  (63 shorter events, 5.0 us)
Async XLA Ops:
  7.2 51.6 %all-gather.6.cloned.1.call-start = ((), (), s32[]{:S(2)}) async-start(), calls=%async_computation.1 | async-start | bytes 1179648 | tf_op jit(solution)/shard_map/all_gather | solution.py:68
  14.5 61.2 %all-gather.4.cloned.1.call-start = ((), (), s32[]{:S(2)}) async-start(), calls=%async_computation | async-start | bytes 1310720 | tf_op jit(solution)/shard_map/all_gather | solution.py:71
  14.6 2.3 copy-start.2
  16.8 42.1 %copy-start.8 = (s32[32]{0:T(128)S(1)}, s32[32]{0:T(128)}, u32[]{:S(2)}) copy-start(s32[32]{0:T(128)} %param.9) | copy-start | bytes 388
  16.9 42.7 %copy-start.6 = (bf16[2048,256]{1,0:T(8,128)(2,1)S(1)}, bf16[2048,256]{1,0:T(8,128)(2,1)}, u32[]{:S(2)}) copy-start(bf16[2048,256]{1,0:T(8,128)(2,1)} %param.7) | copy-start | bytes 3145732
  53.1 58.6 %all-gather.8.cloned.1.call-start = ((), (), s32[]{:S(2)}) async-start(), calls=%async_computation.2 | async-start | bytes 5242880 | tf_op jit(solution)/shard_map/all_gather | solution.py:72
  58.8 304.7 %all-reduce.4.cloned.1.call-start = ((), (), s32[]{:S(2)}) async-start(), calls=%async_computation.3 | async-start | bytes 5242880 | tf_op jit(solution)/shard_map/psum | solution.py:14
  119.7 3.8 copy-start.4
  140.8 1.0 copy-start.3
  297.7 3.0 copy-start.7
  299.4 1.3 copy-start
  299.4 2.3 copy-start.5
  303.4 180.3 %all-reduce.6.cloned.1.call-start = ((), (), s32[]{:S(2)}) async-start(), calls=%async_computation.4 | async-start | bytes 5242880 | tf_op jit(solution)/shard_map/psum | solution.py:15
  485.9 5.9 %copy-start.1 = (bf16[512,2048]{1,0:T(8,128)(2,1)S(1)}, bf16[512,2048]{1,0:T(8,128)(2,1)}, u32[]{:S(2)}) copy-start(bf16[512,2048]{1,0:T(8,128)(2,1)} %copy-done) | copy-start | bytes 6291460
Sparse Core Ops, SparseCore 0:
  14.7 44.0 all-gather.5
  60.3 15.3 all-gather.3
  77.3 34.4 all-gather.7
  303.6 59.8 all-reduce.3
  367.0 116.6 all-reduce.5
